TPU v7x, 32 devices: a whole 2x2x4 slice. The times are simulated.
32 devices in a mesh: groups: 2 (over y), ctx: 4 (over z), head: 2 (over x), pair: 2 (over core).
Axes of the slice: x: 2, y: 2, z: 4, core: 2. Of those that a mesh axis runs over, the one named last changes fastest.
Arguments:
- q_raw: bfloat16 [4096, 2048], P(('groups', 'ctx', 'pair'), 'head'), parts along dimension 0, may hold values from -6 to 6
- k_raw: bfloat16 [4096, 2048], P(('groups', 'ctx', 'pair'), 'head'), parts along dimension 0, may hold values from -6 to 6
- v_raw: bfloat16 [4096, 4096], P(('groups', 'ctx', 'pair'), 'head'), parts along dimension 0, may hold values from -6 to 6
- beta_logit: bfloat16 [32, 4096], P('head', ('groups', 'ctx', 'pair')), parts along dimension 1, may hold values from -6 to 6
- gate_logit: bfloat16 [32, 4096], P('head', ('groups', 'ctx', 'pair')), parts along dimension 1, may hold values from -4 to 13
- out_grad: bfloat16 [4096, 4096], P(('groups', 'ctx', 'pair'), 'head'), parts along dimension 0, may hold values from -6 to 6
- conv_q: bfloat16 [4, 2048], P(None, 'head'), may hold values from -3 to 3
- conv_k: bfloat16 [4, 2048], P(None, 'head'), may hold values from -3 to 3
- conv_v: bfloat16 [4, 4096], P(None, 'head'), may hold values from -3 to 3
- a_log: float32 [32], P('head'), may hold values from 0 to 2.77
- dt_bias: float32 [32], P('head'), may hold values from -16 to -2.9
- doc_ids: int32 [4096], P(('groups', 'ctx', 'pair')), parts along dimension 0, may hold values from 0 to 7, never falling along the last dimension, each value on 1 to 512 neighbouring positions
- swap_blocks: int32 [8], P(('groups', 'ctx')), parts along dimension 0, may hold values from 0 to 1, as said below
Outputs:
- layer_out: bfloat16 [4096, 4096], P(('groups', 'ctx', 'pair'), 'head'), parts along dimension 0
- q_grad: bfloat16 [4096, 2048], P(('groups', 'ctx', 'pair'), 'head'), parts along dimension 0
- k_grad: bfloat16 [4096, 2048], P(('groups', 'ctx', 'pair'), 'head'), parts along dimension 0
- v_grad: bfloat16 [4096, 4096], P(('groups', 'ctx', 'pair'), 'head'), parts along dimension 0
- beta_grad: bfloat16 [32, 4096], P('head', ('groups', 'ctx', 'pair')), parts along dimension 1
- gate_grad: bfloat16 [32, 4096], P('head', ('groups', 'ctx', 'pair')), parts along dimension 1
There are 2 independent parts, one for each index of `groups`. A program takes and returns all parts, laid end to end along the dimension named above; an argument that names none is the same for every part. Nothing has to cross between parts.
Inputs may be any that keep to these rules, and one draw needn't show every extreme that they name: `doc_ids`: document numbers start at 0 and never fall along the tokens; each document has 1 to 512 tokens, one exactly 512. `swap_blocks`: 1 occurs at some context index.
All inputs are finite; a program needn't handle non-finite values.
Results may differ from a plain program's by a relative error of at most 0.001.
Values may be sent and summed in bfloat16 or wider, within the bound.
A program may use at most 320 MiB of HBM per device.

v0:
```python
import math

import jax
import jax.numpy as jnp
from jax import lax
from jax.sharding import PartitionSpec as P

DK = 128
DV = 128
TAPS = 4
CH = 128
SWAP = 128


highest = lax.Precision.HIGHEST
normalizer_guard = 1e-06


def partner_2(value, axis, distance):
    mask = 2**distance
    pairs = [(source, source ^ mask) for source in range(lax.axis_size(axis))]
    return lax.ppermute(value, axis, pairs)


def shifted(array, axis, by):
    peers = lax.axis_size(axis)
    pairs = [(i, i + by) for i in range(peers) if 0 <= i + by < peers]
    return lax.ppermute(array, axis, pairs)


def carried_in(value, axis, join, neutral, backward):
    count, mine = (lax.axis_size(axis), lax.axis_index(axis))
    pieces = jax.tree.map(lambda part: lax.all_gather(part, axis), value)
    if backward:
        pieces = jax.tree.map(lambda part: part[::-1], pieces)
        mine = count - 1 - mine
    total = jax.tree.map(
        lambda part, zero: jnp.full_like(part, 0) + jnp.asarray(zero, part.dtype), value, neutral
    )

    def turn(position, total):
        longer = join(total, jax.tree.map(lambda part: part[position], pieces))
        return jax.tree.map(lambda new, old: jnp.where(position < mine, new, old), longer, total)

    return lax.fori_loop(0, count - 1, turn, total)


def product(left_matrix, right_matrix):
    return jnp.matmul(left_matrix, right_matrix, precision=highest)


def lower_solve(strict_lower, right_side):
    return jax.scipy.linalg.solve_triangular(
        strict_lower, right_side, lower=True, unit_diagonal=True
    )


def conv_silu(extended, weight, ext_ids):
    tap_count = weight.shape[0]
    out_rows = extended.shape[0] - tap_count + 1
    current = ext_ids[tap_count - 1 :]
    summed = jnp.zeros((out_rows, extended.shape[1]), jnp.float32)
    for tap_index in range(tap_count):
        same_doc = (ext_ids[tap_index : tap_index + out_rows] == current).astype(jnp.float32)
        summed = (
            summed
            + weight[tap_index].astype(jnp.float32)
            * extended[tap_index : tap_index + out_rows]
            * same_doc[:, None]
        )
    return jax.nn.silu(summed)


def unit_rows(values, head_width):
    shaped = values.reshape(values.shape[0], -1, head_width)
    return shaped / jnp.sqrt(jnp.sum(shaped * shaped, axis=-1, keepdims=True) + normalizer_guard)


def span_pieces(queries, key_rows, values, beta_rate, decay_log, doc_index, before_doc):
    span_len = queries.shape[0]
    positions = jnp.arange(span_len)
    at_or_below = positions[:, None] >= positions[None, :]
    strictly_below = positions[:, None] > positions[None, :]
    cumulative = jnp.cumsum(decay_log)
    same_doc = (doc_index[:, None] == doc_index[None, :]) & at_or_below
    decay_table = jnp.where(
        same_doc, jnp.exp(jnp.where(same_doc, cumulative[:, None] - cumulative[None, :], 0.0)), 0.0
    )
    start_decay = jnp.where(doc_index == before_doc, jnp.exp(cumulative), 0.0)
    strict_part = jnp.where(
        strictly_below, beta_rate[:, None] * decay_table * product(key_rows, key_rows.T), 0.0
    )
    right_side = jnp.concatenate(
        [beta_rate[:, None] * values, (beta_rate * start_decay)[:, None] * key_rows], axis=1
    )
    solved = lower_solve(strict_part, right_side)
    scores = decay_table * product(queries, key_rows.T)
    weighted = key_rows * decay_table[span_len - 1][:, None]
    value_width = values.shape[1]
    return (
        scores,
        solved[:, :value_width],
        solved[:, value_width:],
        start_decay,
        queries,
        weighted,
    )


def span_step(carried, pieces):
    scores, base_update, correction, start_decay, queries, weighted = pieces
    updates = base_update - product(correction, carried)
    outputs = start_decay[:, None] * product(queries, carried) + product(scores, updates)
    new_state = start_decay[-1] * carried + product(weighted.T, updates)
    return (new_state, outputs)


def compose_maps(earlier, later):
    return (product(later[0], earlier[0]), product(later[0], earlier[1]) + later[1])


def span_maps(span_piece, unit_matrix):
    scores, base_update, correction, start_decay, queries, weighted = span_piece
    weighted_t = jnp.swapaxes(weighted, 1, 2)
    span_map = start_decay[:, -1][:, None, None] * unit_matrix - product(weighted_t, correction)
    span_add = product(weighted_t, base_update)
    return (span_map, span_add)


def restore(mine, partner, core_index, moved_rows, token_axis):
    extent = mine.shape[token_axis]
    view_shape = [1] * mine.ndim
    view_shape[token_axis] = extent
    positions = jnp.arange(extent, dtype=jnp.int32).reshape(tuple(view_shape))
    first_core = core_index == 0
    roll_by = jnp.where(first_core, extent - moved_rows, moved_rows)
    from_partner = jnp.where(first_core, positions >= extent - moved_rows, positions < moved_rows)
    return jnp.where(from_partner, jnp.roll(partner, roll_by, axis=token_axis), mine)


def body(
    q_raw,
    k_raw,
    v_raw,
    beta_logit,
    gate_logit,
    out_grad,
    conv_q,
    conv_k,
    conv_v,
    a_log,
    dt_bias,
    doc_ids,
    swap_blocks,
):
    rows_dev = q_raw.shape[0]
    core_index = lax.axis_index("pair")
    moved_rows = swap_blocks[0] * SWAP
    partner = partner_2((q_raw, k_raw, v_raw, out_grad, beta_logit, gate_logit), "pair", 0)
    q_seq = restore(q_raw, partner[0], core_index, moved_rows, 0)
    k_seq = restore(k_raw, partner[1], core_index, moved_rows, 0)
    v_seq = restore(v_raw, partner[2], core_index, moved_rows, 0)
    grad_seq = restore(out_grad, partner[3], core_index, moved_rows, 0)
    beta_seq = restore(beta_logit, partner[4], core_index, moved_rows, 1)
    gate_seq = restore(gate_logit, partner[5], core_index, moved_rows, 1)
    tail_len = TAPS - 1
    ids_half = doc_ids.astype(jnp.bfloat16)
    before = shifted(
        (
            q_seq[rows_dev - tail_len :],
            k_seq[rows_dev - tail_len :],
            v_seq[rows_dev - tail_len :],
            ids_half[rows_dev - tail_len :],
        ),
        ("ctx", "pair"),
        1,
    )
    ext_q = jnp.concatenate([before[0], q_seq], axis=0).astype(jnp.float32)
    ext_k = jnp.concatenate([before[1], k_seq], axis=0).astype(jnp.float32)
    ext_v = jnp.concatenate([before[2], v_seq], axis=0).astype(jnp.float32)
    ext_ids = jnp.concatenate([before[3], ids_half]).astype(jnp.float32)
    spans = rows_dev // CH
    doc_now = ext_ids[TAPS - 1 :].reshape(spans, CH)
    doc_before = ext_ids[TAPS - 2 : TAPS - 2 + rows_dev : CH]

    def to_spans(source):
        return source.reshape(spans, CH, source.shape[1], source.shape[2]).transpose(0, 2, 1, 3)

    def rate_spans(source):
        return source.reshape(source.shape[0], spans, CH).transpose(1, 0, 2)

    per_head = jax.vmap(span_pieces, in_axes=(0, 0, 0, 0, 0, None, None))
    all_pieces = jax.checkpoint(jax.vmap(per_head))

    def prepare(query_raw, key_raw, value_raw, beta_in, gate_in):
        queries = unit_rows(conv_silu(query_raw, conv_q, ext_ids), DK) / math.sqrt(DK)
        key_rows = unit_rows(conv_silu(key_raw, conv_k, ext_ids), DK)
        value_rows = conv_silu(value_raw, conv_v, ext_ids).reshape(rows_dev, -1, DV)
        group_size = value_rows.shape[1] // queries.shape[1]
        queries = jnp.repeat(queries, group_size, axis=1)
        key_rows = jnp.repeat(key_rows, group_size, axis=1)
        beta_rate = jax.nn.sigmoid(beta_in)
        decay_log = -jnp.exp(a_log)[:, None] * jax.nn.softplus(gate_in + dt_bias[:, None])
        pieces = all_pieces(
            to_spans(queries),
            to_spans(key_rows),
            to_spans(value_rows),
            rate_spans(beta_rate),
            rate_spans(decay_log),
            doc_now,
            doc_before,
        )
        head_count = value_rows.shape[1]
        unit_matrix = jnp.broadcast_to(jnp.eye(DK, dtype=jnp.float32), (head_count, DK, DK))

        def compose_span(carry_maps, span_piece):
            return (compose_maps(carry_maps, span_maps(span_piece, unit_matrix)), None)

        summary, unused = lax.scan(
            compose_span, (unit_matrix, jnp.zeros((head_count, DK, DV), jnp.float32)), pieces
        )
        return (pieces, summary[0], summary[1])

    prepared, pull_prepare = jax.vjp(
        prepare, ext_q, ext_k, ext_v, beta_seq.astype(jnp.float32), gate_seq.astype(jnp.float32)
    )
    pieces, transition, offset = prepared
    identity = (
        jnp.broadcast_to(jnp.eye(DK, dtype=jnp.float32), transition.shape),
        jnp.zeros_like(offset),
    )
    prefix = carried_in((transition, offset), ("ctx", "pair"), compose_maps, identity, False)
    state_in = prefix[1]

    def chain(pieces_in, start_state):

        def advance(carried, span_piece):
            return jax.vmap(span_step)(carried, span_piece)

        final_state, outputs = lax.scan(advance, start_state, pieces_in)
        return outputs

    outputs, pull_chain = jax.vjp(chain, pieces, state_in)
    layer_out = outputs.transpose(0, 2, 1, 3).reshape(rows_dev, -1)
    head_count = transition.shape[0]
    grad_spans = (
        grad_seq.astype(jnp.float32).reshape(spans, CH, head_count, DV).transpose(0, 2, 1, 3)
    )
    piece_grads, carry_grad = pull_chain(grad_spans)
    flipped = jnp.swapaxes(transition, 1, 2)
    suffix = carried_in((flipped, carry_grad), ("ctx", "pair"), compose_maps, identity, True)
    grad_out = suffix[1]
    transition_grad = product(grad_out, jnp.swapaxes(state_in, 1, 2))
    input_grads = pull_prepare((piece_grads, transition_grad, grad_out))
    spilled = shifted(
        (input_grads[0][:tail_len], input_grads[1][:tail_len], input_grads[2][:tail_len]),
        ("ctx", "pair"),
        -1,
    )
    pad_rows = ((rows_dev - tail_len, 0), (0, 0))
    q_grad = input_grads[0][tail_len:] + jnp.pad(spilled[0], pad_rows)
    k_grad = input_grads[1][tail_len:] + jnp.pad(spilled[1], pad_rows)
    v_grad = input_grads[2][tail_len:] + jnp.pad(spilled[2], pad_rows)
    return (
        layer_out.astype(jnp.bfloat16),
        q_grad.astype(jnp.bfloat16),
        k_grad.astype(jnp.bfloat16),
        v_grad.astype(jnp.bfloat16),
        input_grads[3].astype(jnp.bfloat16),
        input_grads[4].astype(jnp.bfloat16),
    )


def solution(mesh):
    return jax.shard_map(
        body,
        mesh=mesh,
        in_specs=(
            P(("groups", "ctx", "pair"), "head"),
            P(("groups", "ctx", "pair"), "head"),
            P(("groups", "ctx", "pair"), "head"),
            P("head", ("groups", "ctx", "pair")),
            P("head", ("groups", "ctx", "pair")),
            P(("groups", "ctx", "pair"), "head"),
            P(None, "head"),
            P(None, "head"),
            P(None, "head"),
            P("head"),
            P("head"),
            P(("groups", "ctx", "pair")),
            P(("groups", "ctx")),
        ),
        out_specs=(
            P(("groups", "ctx", "pair"), "head"),
            P(("groups", "ctx", "pair"), "head"),
            P(("groups", "ctx", "pair"), "head"),
            P(("groups", "ctx", "pair"), "head"),
            P("head", ("groups", "ctx", "pair")),
            P("head", ("groups", "ctx", "pair")),
        ),
        check_vma=False,
    )
```

profile of v0, /device:TPU:1, one launch (start us, length us, event | category | flops | bytes accessed | tf_op | source)
XLA Modules:
  0.0 1318.4 jit_solution(9043184303846461592)
XLA Ops:
  36.4 5.5 convert_bitcast_fusion
  47.6 6.0 add_bitcast_fusion
  53.6 315.8 %custom-call.16 = f32[2,16,1,128,128]{3,4,2,1,0:T(8,128)} custom-call(f32[2,16,1,128,128]{4,3,2,1,0:T(8,128)} %add_bitcast_fusion), custom_call_target="InvertDiagBlocksLowerTriangular" | custom-call | tf_op jit(solution)/shard_map/jvp(vmap(vmap(jit(_solve_triangular))))/triangular_solve/custom-call.1 | solution.py:53
  380.2 6.6 fusion.135
  395.9 24.0 %while.127 = (s32[]{:T(128)}, f32[16,128,128]{2,1,0:T(8,128)S(1)}, f32[16,128,128]{2,1,0:T(8,128)}, f32[2,16,128,128]{3,2,1,0:T(8,128)}, f32[2,16,128,128]{3,2,1...) while((s32[]{:T(128)}, f32[16,128,128]{2,1,0:T(8,128)S(1)}, ...), condition=%wide.region_3.8_spmd.clone, body=%wide.region_2.7_spmd.clone.sunk | while | flops 1611923456 | bytes 65097160 | solution.py:219
  442.4 5.9 fusion.173
  450.6 51.5 %all-gather.9.cloned.1.call-done = f32[128,128,128]{2,1,0:T(8,128)} async-done(((f32[16,128,128]{2,1,0:T(8,128)}), f32[128,128,128]{2,1,0:T(8,128)}) %all-gather.9.cloned.1.call-update) | async-done | bytes 8388624 | tf_op jit(solution)/shard_map/all_gather | solution.py:33
  502.1 83.5 %all-gather.11.cloned.1.call-done = f32[128,128,128]{2,1,0:T(8,128)} async-done(((f32[16,128,128]{2,1,0:T(8,128)}), f32[128,128,128]{2,1,0:T(8,128)}) %all-gather.11.cloned.1.call-update) | async-done | bytes 8388624 | tf_op jit(solution)/shard_map/all_gather | solution.py:33
  585.6 21.1 %while.128 = (s32[]{:T(128)}, f32[16,128,128]{2,1,0:T(8,128)S(1)}, s32[]{:T(128)}, f32[8,16,128,128]{3,2,1,0:T(8,128)}, f32[8,16,128,128]{3,2,1,0:T(8,128)}, /*index=5*/s32[]{:T(128)}, s32[]{:T(128)}) while((s32[]{:T(128)}, f32[16,128,128]{2,1,0:T(8,128)S(1)}, s32[]{:T(128)}, f32[8,16,128,128]{3,2,1,0:T(8,128)}, ...), condition=%wide.region_5.10_spmd.clone, body=%wide.region_4.9_spmd.clone.sunk | while | flops 403701760 | bytes 7342695 | solution.py:45
  613.1 25.1 %while.125 = (s32[]{:T(128)}, f32[16,128,128]{2,1,0:T(8,128)S(1)}, bf16[2,16,128,128]{3,2,1,0:T(8,128)(2,1)}, f32[2,16,128,128]{3,2,1,0:T(8,128)}, f32[2,16,128,...) while((s32[]{:T(128)}, f32[16,128,128]{2,1,0:T(8,128)S(1)}, ...), condition=%wide.region_8.13_spmd, body=%wide.region_7.12_spmd.sunk | while | flops 1611923456 | bytes 72438744 | solution.py:240
  646.3 55.0 %while.129 = (s32[]{:T(128)}, f32[16,128,128]{2,1,0:T(8,128)S(1)}, f32[2,16,128,128]{3,2,1,0:T(8,128)}, f32[2,16,128,128]{3,2,1,0:T(8,128)}, f32[2,16,128,128]{3...) while((s32[]{:T(128)}, f32[16,128,128]{2,1,0:T(8,128)S(1)}, ...), condition=%wide.region_12.17_spmd.clone, body=%wide.region_9.16_spmd.clone.sunk | while | flops 3225419776 | bytes 134293392 | solution.py:240
  702.4 5.1 copy_bitcast_fusion.1
  709.5 8.5 rev.6
  718.0 64.7 %all-gather.15.cloned.1.call-done = f32[128,128,128]{2,1,0:T(8,128)} async-done(((f32[16,128,128]{2,1,0:T(8,128)}), f32[128,128,128]{2,1,0:T(8,128)}) %all-gather.15.cloned.1.call-update) | async-done | bytes 8388624 | tf_op jit(solution)/shard_map/all_gather | solution.py:33
  782.8 7.9 rev.7
  790.6 20.4 %while.130 = (s32[]{:T(128)}, f32[16,128,128]{2,1,0:T(8,128)S(1)}, s32[]{:T(128)}, f32[8,16,128,128]{3,2,1,0:T(8,128)}, f32[8,16,128,128]{3,2,1,0:T(8,128)}, /*index=5*/s32[]{:T(128)}, s32[]{:T(128)}) while((s32[]{:T(128)}, f32[16,128,128]{2,1,0:T(8,128)S(1)}, s32[]{:T(128)}, f32[8,16,128,128]{3,2,1,0:T(8,128)}, ...), condition=%wide.region_14.19_spmd.clone, body=%wide.region_13.18_spmd.clone.sunk | while | flops 403701760 | bytes 7342695 | solution.py:45
  819.1 50.8 %while.126 = (s32[]{:T(128)}, f32[16,128,128]{2,1,0:T(8,128)}, f32[16,128,128]{2,1,0:T(8,128)}, f32[2,16,128,128]{3,2,1,0:T(8,128)}, f32[2,16,128,128]{3,2,1,0:T...) while((s32[]{:T(128)}, f32[16,128,128]{2,1,0:T(8,128)}, ...), condition=%wide.region_17.22_spmd.clone, body=%wide.region_15.21_spmd.clone.sunk | while | flops 3222798336 | bytes 111259240 | solution.py:219
  879.4 5.7 fusion.253
  889.2 315.8 %custom-call.10 = f32[2,16,1,128,128]{3,4,2,1,0:T(8,128)} custom-call(f32[2,16,1,128,128]{4,3,2,1,0:T(8,128)} %add_bitcast_fusion.2), custom_call_target="InvertDiagBlocksLowerTriangular" | custom-call | tf_op jit(solution)/shard_map/transpose(jvp(jvp()))/checkpoint/vmap(vmap(jit(_solve_triangular)))/triangular_solve | solution.py:53
  1205.2 7.4 fusion.144
  1225.8 4.9 multiply_reduce_fusion.2
  1238.3 6.4 add_bitcast_fusion.1
  1254.5 5.4 add_bitcast_fusion.3
  1292.1 6.0 fusion.242
  (689 shorter events, 386.3 us)
Async XLA Ops:
  7.2 494.9 %all-gather.9.cloned.1.call-start = ((), (), s32[]{:S(2)}) async-start(), calls=%async_computation | async-start | bytes 9437184 | tf_op jit(solution)/shard_map/all_gather | solution.py:33
  7.3 12.0 collective-permute-start.1
  7.4 12.3 collective-permute-start.4
  8.6 9.4 collective-permute-start
  14.5 7.2 collective-permute-start.7
  15.8 5.9 collective-permute-start.2
  17.8 352.6 %copy-start.106 = (f32[1,2048]{1,0:T(1,128)}, f32[1,2048]{1,0:T(1,128)S(1)}, u32[]{:S(2)}) copy-start(f32[1,2048]{1,0:T(1,128)S(1)} %get-tuple-element.1833) | copy-start | bytes 24580
  17.9 352.6 %copy-start.108 = (f32[1,2048]{1,0:T(1,128)}, f32[1,2048]{1,0:T(1,128)S(1)}, u32[]{:S(2)}) copy-start(f32[1,2048]{1,0:T(1,128)S(1)} %get-tuple-element.1831) | copy-start | bytes 24580
  17.9 352.6 %copy-start.110 = (f32[1,2048]{1,0:T(1,128)}, f32[1,2048]{1,0:T(1,128)S(1)}, u32[]{:S(2)}) copy-start(f32[1,2048]{1,0:T(1,128)S(1)} %get-tuple-element.1832) | copy-start | bytes 24580
  17.9 352.6 %copy-start.112 = (f32[1,2048]{1,0:T(1,128)}, f32[1,2048]{1,0:T(1,128)S(1)}, u32[]{:S(2)}) copy-start(f32[1,2048]{1,0:T(1,128)S(1)} %get-tuple-element.1834) | copy-start | bytes 24580
  18.0 18.4 %collective-permute-start.9 = (bf16[256,2048]{1,0:T(8,128)(2,1)}, bf16[256,2048]{1,0:T(8,128)(2,1)}, u32[]{:S(2)}, u32[]{:S(2)}) collective-permute-start(bf16[256,2048]{1,0:T(8,128)(2,1)} %param.38), channel_id=1, source_target_pairs={{0,1},{1,0},{2,3},{3,2},{4,5},{5,4},{6,7},{7,6},{8,9},{9,8},{10,11... | collective-permute-start | bytes 3145736 | tf_op jit(solution)/shard_map/ppermute | solution.py:22
  19.2 17.1 %collective-permute-start.5 = (bf16[256,2048]{1,0:T(8,128)(2,1)}, bf16[256,2048]{1,0:T(8,128)(2,1)}, u32[]{:S(2)}, u32[]{:S(2)}) collective-permute-start(bf16[256,2048]{1,0:T(8,128)(2,1)} %param.35), channel_id=1, source_target_pairs={{0,1},{1,0},{2,3},{3,2},{4,5},{5,4},{6,7},{7,6},{8,9},{9,8},{10,11... | collective-permute-start | bytes 3145736 | tf_op jit(solution)/shard_map/ppermute | solution.py:22
  25.2 6.8 collective-permute-start.3
  29.3 344.8 %copy-start.86 = (f32[2,2,8,128]{3,2,0,1:T(8,128)}, f32[2,2,8,128]{3,2,0,1:T(8,128)S(1)}, u32[]{:S(2)}) copy-start(f32[2,2,8,128]{3,2,0,1:T(8,128)S(1)} %copy.517) | copy-start | bytes 49156
  42.5 326.9 %collective-permute-start.6 = (bf16[3,2048]{1,0:T(4,128)(2,1)}, bf16[3,2048]{1,0:T(4,128)(2,1)}, u32[]{:S(2)}, u32[]{:S(2)}) collective-permute-start(bf16[3,2048]{1,0:T(4,128)(2,1)} %slice.213), channel_id=1, source_target_pairs={{0,1},{1,4},{4,5},{5,8},{8,9},{9,12},{12,13},{2,3},{3,6},{6,7},{7,... | collective-permute-start | bytes 36872 | tf_op jit(solution)/shard_map/ppermute | solution.py:28
  47.6 326.5 %copy-start.35 = (f32[256,8,2,128]{3,0,2,1:T(8,128)}, f32[256,8,2,128]{3,0,2,1:T(8,128)S(1)}, u32[]{:S(2)}) copy-start(f32[256,8,2,128]{3,0,2,1:T(8,128)S(1)} %broadcast_in_dim.323) | copy-start | bytes 6291460
  420.9 164.7 %all-gather.11.cloned.1.call-start = ((), (), s32[]{:S(2)}) async-start(), calls=%async_computation.1 | async-start | bytes 9437184 | tf_op jit(solution)/shard_map/all_gather | solution.py:33
  421.6 287.9 %all-gather.13.cloned.1.call-start = ((), (), s32[]{:S(2)}) async-start(), calls=%async_computation.2 | async-start | bytes 9437184 | tf_op jit(solution)/shard_map/all_gather | solution.py:33
  424.3 358.5 %all-gather.15.cloned.1.call-start = ((), (), s32[]{:S(2)}) async-start(), calls=%async_computation.3 | async-start | bytes 9437184 | tf_op jit(solution)/shard_map/all_gather | solution.py:33
  424.6 7.3 collective-permute-start.8
  885.7 319.4 %copy-start.164 = (f32[2]{0:T(128)S(1)}, f32[2]{0:T(128)}, u32[]{:S(2)}) copy-start(f32[2]{0:T(128)} %copy-done.163) | copy-start | bytes 28
  1284.3 21.0 %collective-permute-start.10 = (f32[3,1024]{0,1:T(8,128)}, f32[3,1024]{0,1:T(8,128)}, u32[]{:S(2)}, u32[]{:S(2)}) collective-permute-start(f32[3,1024]{0,1:T(8,128)} %pad_add_fusion.7), channel_id=1, source_target_pairs={{1,0},{4,1},{5,4},{8,5},{9,8},{12,9},{13,12},{3,2},{6,3},{7,6},{10... | collective-permute-start | bytes 36872 | tf_op jit(solution)/shard_map/ppermute | solution.py:28
  1288.0 18.8 %collective-permute-start.11 = (f32[3,1024]{0,1:T(8,128)}, f32[3,1024]{0,1:T(8,128)}, u32[]{:S(2)}, u32[]{:S(2)}) collective-permute-start(f32[3,1024]{0,1:T(8,128)} %pad_add_fusion.6), channel_id=1, source_target_pairs={{1,0},{4,1},{5,4},{8,5},{9,8},{12,9},{13,12},{3,2},{6,3},{7,6},{10... | collective-permute-start | bytes 36872 | tf_op jit(solution)/shard_map/ppermute | solution.py:28
  1290.0 20.4 %collective-permute-start.12 = (f32[3,2048]{1,0:T(4,128)S(1)}, f32[3,2048]{1,0:T(4,128)S(1)}, u32[]{:S(2)}, u32[]{:S(2)}) collective-permute-start(f32[3,2048]{1,0:T(4,128)S(1)} %pad_add_fusion.8), channel_id=1, source_target_pairs={{1,0},{4,1},{5,4},{8,5},{9,8},{12,9},{13,12},{3,2},{6,3},{7,6},{10... | collective-permute-start | bytes 73736 | tf_op jit(solution)/shard_map/ppermute | solution.py:28
  (194 other events, 2164.7 us)
Sparse Core Ops, SparseCore 0:
  421.0 81.0 all-gather.8
  504.3 81.2 all-gather.10
  587.2 80.5 all-gather.12
  702.4 80.2 all-gather.14
where the time goes:
time: 1330 us; the launch traced here: 1320 us
  other arithmetic  723 us (54%)
  matrix products  233 us (18%)
  waiting for transfers between devices  207 us (16%)
  local copies, waits for them, and re-layouts  112 us (8%)
  starting transfers between devices  23.2 us (2%)
  between operations  16.6 us (1%)
    another operation x6, other arithmetic, lower_solve(): jax.scipy.linalg.solve_triangular(strict_lower, right_side, lower=True, u...  635 us
    dot_general x71, matrix products, product(): return jnp.matmul(left_matrix, right_matrix, precision=highest)  205 us
    all_gather x4, waiting for transfers between devices, carried_in(): pieces = jax.tree.map(lambda part: lax.all_gather(part, axis), value)  200 us
  transfers between devices with their start and end apart: 17, of which 5 were waited for; matrix products, arithmetic and copies ran while one was open for 38% of the time, Pallas kernels for 0%

commit v1 on v0

v1 whole, which is shorter than its diff:
```python
import functools
import math

import jax
import jax.numpy as jnp
from jax import lax
from jax.experimental import pallas as pl
from jax.experimental.pallas import tpu as pltpu
from jax.sharding import PartitionSpec as P

DK = 128
TAPS = 4
CH = 128
SWAP = 128
HALO = 8
GUARD = 1e-06
SCALE = 1.0 / math.sqrt(DK)
DOC_PARTS = 4

f32 = jnp.float32
bf16 = jnp.bfloat16
highest = lax.Precision.HIGHEST
SEQ = ("ctx", "pair")


def split(x):
    high = x.astype(bf16)
    return high, (x - high.astype(f32)).astype(bf16)


def mm(a, b):
    ah, al = split(a)
    bh, bl = split(b)
    lhs = jnp.concatenate([ah, al], axis=1)
    rhs = jnp.concatenate(
        [jnp.concatenate([bh, bl], axis=1), jnp.concatenate([bh, jnp.zeros_like(bh)], axis=1)], axis=0
    )
    r = lax.dot_general(lhs, rhs, (((1,), (0,)), ((), ())), preferred_element_type=f32)
    n = b.shape[1]
    return r[:, :n] + r[:, n:]


def mm_nt(a, b):
    ah, al = split(a)
    bh, bl = split(b)
    lhs = jnp.concatenate([ah, al], axis=1)
    rhs = jnp.concatenate(
        [jnp.concatenate([bh, bh], axis=1), jnp.concatenate([bl, jnp.zeros_like(bl)], axis=1)], axis=0
    )
    r = lax.dot_general(lhs, rhs, (((1,), (1,)), ((), ())), preferred_element_type=f32)
    n = b.shape[0]
    return r[:, :n] + r[:, n:]


def iota(axis):
    return lax.broadcasted_iota(jnp.int32, (CH, CH), axis)


def rowsum(x):
    return jnp.sum(x, axis=1, keepdims=True)


def columns(rows):
    return jnp.concatenate([rows, jnp.zeros((CH - rows.shape[0], CH), f32)], axis=0).T


def sigmoid(a):
    return 1.0 / (1.0 + jnp.exp(-a))


def fetch(raw, recv, flags):
    first = raw[:SWAP, :]
    second = raw[SWAP:, :]
    got = recv[...]
    first = jnp.where(flags[0] > 0, got, first)
    second = jnp.where(flags[1] > 0, got, second)
    return jnp.concatenate([first, second], axis=0)


def conv(x, halo, taps, masks):
    ext = jnp.concatenate([halo, x], axis=0)
    width = x.shape[1] // CH
    total = taps[TAPS - 1 : TAPS, :] * x
    for d in range(1, TAPS):
        moved = pltpu.roll(ext, d, 0)[HALO:, :]
        mask = masks[d - 1]
        if width > 1:
            mask = jnp.concatenate([mask] * width, axis=1)
        total = total + taps[TAPS - 1 - d : TAPS - d, :] * (moved * mask)
    return total


def conv_back(da, taps, masks):
    width = da.shape[1] // CH
    zeros = jnp.zeros((HALO, da.shape[1]), f32)
    total = taps[TAPS - 1 : TAPS, :] * jnp.concatenate([da, zeros], axis=0)
    size = total.shape[0]
    for d in range(1, TAPS):
        mask = masks[d - 1]
        if width > 1:
            mask = jnp.concatenate([mask] * width, axis=1)
        ext = jnp.concatenate([da * mask, zeros], axis=0)
        total = total + taps[TAPS - 1 - d : TAPS - d, :] * pltpu.roll(ext, size - d, 0)
    return total


def local_maps(
    flags, q_raw, k_raw, v_raw, g_raw, q_got, k_got, v_got, g_got, q_halo, k_halo, v_halo,
    q_taps, k_taps, v_taps, masks, docs, rows,
    a_q, a_k, a_v, qn_out, kn_out, seq_grad, inv_out, kk_out, qk_out, pdo_out,
):
    blocks = q_raw.shape[0] // CH
    qa = conv(fetch(q_raw, q_got, flags).astype(f32), q_halo[...], q_taps, masks)
    ka = conv(fetch(k_raw, k_got, flags).astype(f32), k_halo[...], k_taps, masks)
    va = conv(fetch(v_raw, v_got, flags).astype(f32), v_halo[...], v_taps, masks)
    a_q[...] = qa
    a_k[...] = ka
    a_v[...] = va
    gs = fetch(g_raw, g_got, flags)
    seq_grad[...] = gs
    do_all = gs.astype(f32)
    qu = qa * sigmoid(qa)
    ku = ka * sigmoid(ka)
    v_all = va * sigmoid(va)
    qn = qu * (SCALE / jnp.sqrt(rowsum(qu * qu) + GUARD))
    kn = ku * (1.0 / jnp.sqrt(rowsum(ku * ku) + GUARD))
    qn_out[...] = qn
    kn_out[...] = kn
    row, col = iota(0), iota(1)
    eye = (row == col).astype(f32)
    heads = v_raw.shape[1] // CH
    state = []
    for n in range(blocks):
        q = qn[n * CH : (n + 1) * CH]
        k = kn[n * CH : (n + 1) * CH]
        both = mm_nt(jnp.concatenate([k, q], axis=0), k)
        kk, qk = both[:CH], both[CH:]
        kk_out[0, n] = kk
        qk_out[0, n] = qk
        q_t, k_t = q.T, k.T
        flat = rows[0, n]
        cols = columns(flat)
        for e in range(heads):
            beta, c, s, w = [cols[:, 4 * e + i : 4 * e + i + 1] for i in range(4)]
            beta_r, c_r, s_r, w_r = [flat[4 * e + i : 4 * e + i + 1, :] for i in range(4)]
            s_last = s_r[:, CH - 1 :]
            decay = jnp.exp(jnp.minimum(c - c_r, 0.0)) * docs[n]
            low = jnp.where(row > col, beta * decay * kk, 0.0)
            do = do_all[n * CH : (n + 1) * CH, e * CH : (e + 1) * CH]
            v = v_all[n * CH : (n + 1) * CH, e * CH : (e + 1) * CH]
            state.append((n, e, low, decay * qk, do, v, k * w, (beta_r * s_r) * k_t, beta * s * k, s_r * q_t, beta * v, s_last))
    inv = []
    for item in state:
        inv.append(eye - jnp.where((row >> 1) == (col >> 1), item[2], 0.0))
    size = 1
    while (2 << size) <= CH:
        near = ((row >> (size + 1)) == (col >> (size + 1))) & ((row >> size) != (col >> size))
        half = [mm(jnp.where(near, item[2], 0.0), t) for item, t in zip(state, inv)]
        inv = [t - mm(t, h) for t, h in zip(inv, half)]
        size += 1
    maps = {}
    for item, t in zip(state, inv):
        n, e, low, p, do, v, kw, bsk_t, bsk, sq_t, bv, s_last = item
        inv_out[0, e, n] = t
        pdo = mm(p.T, do)
        pdo_out[0, e, n] = pdo
        t_t = t.T
        b = mm(t_t, kw)
        cc = mm(t_t, pdo)
        b_t = b.T
        m = s_last * eye - mm(b_t, bsk)
        a = mm(b_t, bv)
        g = mm(sq_t, do) - mm(bsk_t, cc)
        maps[n, e] = (m, a, g)
    results = []
    for e in range(heads):
        m, a, g = maps[0, e]
        for n in range(1, blocks):
            m2, a2, g2 = maps[n, e]
            g = g + mm(m.T, g2)
            a = mm(m2, a) + a2
            m = mm(m2, m)
        results.append((m, a, g))
    return results


def prepare_kernel(*refs):
    m_out, a_out, g_out = refs[-3:]
    for e, (m, a, g) in enumerate(local_maps(*refs[:-3])):
        m_out[e] = m
        a_out[e] = a
        g_out[e] = g


def exchange_kernel(ctxs, hk, *refs):
    sent, got, kept, kept_map, x_buf, y_buf, y_got, swap_s, swap_r, hop_s, hop_r, pair_s, pair_r = refs[-13:]
    s_out, d_out = refs[-15:-13]
    step = pl.program_id(0)
    core = lax.axis_index("pair")
    ctx = lax.axis_index("ctx")
    first = core == 0
    partner = {"pair": 1 - core}
    peer_ctx = jnp.where(first, ctx - 1, ctx + 1)
    has_peer = (peer_ctx >= 0) & (peer_ctx < ctxs)
    peer = {"ctx": jnp.clip(peer_ctx, 0, ctxs - 1), "pair": 1 - core}
    mesh_id = pl.DeviceIdType.MESH

    def swap(j):
        return pltpu.make_async_remote_copy(
            sent.at[j], got.at[j], swap_s.at[j], swap_r.at[j], device_id=partner, device_id_type=mesh_id
        )

    def hop(j):
        return pltpu.make_async_remote_copy(
            x_buf.at[j], y_buf.at[j], hop_s.at[j], hop_r.at[j], device_id=peer, device_id_type=mesh_id
        )

    def pair(j):
        return pltpu.make_async_remote_copy(
            y_buf.at[j], y_got.at[j], pair_s.at[j], pair_r.at[j], device_id=partner, device_id_type=mesh_id
        )

    @pl.when(step == 0)
    def _():
        barrier = pltpu.get_barrier_semaphore()
        pl.semaphore_signal(barrier, inc=1, device_id=partner, device_id_type=mesh_id)

        @pl.when(has_peer)
        def _():
            pl.semaphore_signal(barrier, inc=1, device_id=peer, device_id_type=mesh_id)

        pl.semaphore_wait(barrier, jnp.where(has_peer, 2, 1))

    @pl.when(step < hk)
    def _():
        for e, (m, a, g) in enumerate(local_maps(*refs[:-15])):
            m_t = m.T
            sent[step, 0, e] = jnp.where(first, a, g)
            sent[step, 1, e] = jnp.where(first, m, m_t)
            kept[step, e] = jnp.where(first, g, a)
            kept_map[step, e] = jnp.where(first, m_t, m)
        swap(step).start()

    @pl.when((step >= 1) & (step < hk + 1))
    def _():
        j = step - 1
        swap(j).wait_recv()
        for e in range(s_out.shape[0]):
            x_buf[j, e] = kept[j, e] + mm(kept_map[j, e], got[j, 0, e])

        @pl.when(has_peer)
        def _():
            hop(j).start()

    @pl.when((step >= 2) & (step < hk + 2))
    def _():
        j = step - 2

        @pl.when(has_peer)
        def _():
            hop(j).wait_recv()

        @pl.when(jnp.logical_not(has_peer))
        def _():
            y_buf[j] = jnp.zeros(y_buf.shape[1:], f32)

        pair(j).start()

    @pl.when(step >= 3)
    def _():
        j = step - 3
        pair(j).wait_recv()
        for e in range(s_out.shape[0]):
            mine = y_buf[j, e]
            other = got[j, 0, e] + mm(got[j, 1, e], y_got[j, e])
            s_out[e] = jnp.where(first, mine, other)
            d_out[e] = jnp.where(first, other, mine)
        swap(j).wait_send()
        pair(j).wait_send()

        @pl.when(has_peer)
        def _():
            hop(j).wait_send()


def join_kernel(m, a, g, a_in, g_in, a_out, g_out):
    for e in range(m.shape[0]):
        here = m[e]
        a_out[e] = a[e] + mm(here, a_in[e])
        g_out[e] = g[e] + mm(here.T, g_in[e])


def norm_back(dy, a, scale):
    sig = sigmoid(a)
    u = a * sig
    inverse = 1.0 / jnp.sqrt(rowsum(u * u) + GUARD)
    y = u * inverse
    dy = dy * scale
    du = (dy - y * rowsum(y * dy)) * inverse
    return du * (sig + u * (1.0 - sig))


def main_kernel(
    a_q, a_k, a_v, qn, kn, seq_grad, inv, kk_in, qk_in, pdo_in, q_taps, k_taps, v_taps, masks, docs, rows,
    s_in, d_in, out, q_grad, k_grad, v_grad, q_end, k_end, v_end, q_spill, k_spill, v_spill, row_grads,
):
    tokens = a_q.shape[0]
    blocks = tokens // CH
    heads = a_v.shape[1] // CH
    row, col = iota(0), iota(1)
    va = a_v[...]
    v_sig = sigmoid(va)
    v_all = va * v_sig
    info = []
    for n in range(blocks):
        q = qn[n * CH : (n + 1) * CH, :]
        k = kn[n * CH : (n + 1) * CH, :]
        info.append((q, k, q.T, k.T, rows[0, n], columns(rows[0, n])))
    fwd = {}
    carried = [s_in[e] for e in range(heads)]
    for n in range(blocks):
        q, k, q_t, k_t, flat, cols = info[n]
        kq = jnp.concatenate([k, q], axis=0)
        for e in range(heads):
            beta, c, s, w = [cols[:, 4 * e + i : 4 * e + i + 1] for i in range(4)]
            beta_r, c_r, s_r, w_r = [flat[4 * e + i : 4 * e + i + 1, :] for i in range(4)]
            s_last = s_r[:, CH - 1 :]
            v = v_all[n * CH : (n + 1) * CH, e * CH : (e + 1) * CH]
            decay = jnp.exp(jnp.minimum(c - c_r, 0.0)) * docs[n]
            p = decay * qk_in[0, n]
            st = carried[e]
            kqs = mm(kq, st)
            ks, qs = kqs[:CH], kqs[CH:]
            t = inv[0, e, n]
            u = mm(t, beta * (v - s * ks))
            o = s * qs + mm(p, u)
            out[n * CH : (n + 1) * CH, e * CH : (e + 1) * CH] = o.astype(bf16)
            if n + 1 < blocks:
                carried[e] = s_last * st + mm(k_t * w_r, u)
            fwd[n, e] = (st, u, qs, decay, p, v)
    grads = [d_in[e] for e in range(heads)]
    dqs, dks, dvs = [None] * blocks, [None] * blocks, {}
    for n in reversed(range(blocks)):
        q, k, q_t, k_t, flat, cols = info[n]
        packed = jnp.zeros((CH, CH), f32)
        dqk_sum = dkk_sum = dq = dk = 0.0
        for e in range(heads):
            beta, c, s, w = [cols[:, 4 * e + i : 4 * e + i + 1] for i in range(4)]
            beta_r, c_r, s_r, w_r = [flat[4 * e + i : 4 * e + i + 1, :] for i in range(4)]
            s_last = s_r[:, CH - 1 :]
            st, u, qs, decay, p, v = fwd[n, e]
            ds_out = grads[e]
            do = seq_grad[n * CH : (n + 1) * CH, e * CH : (e + 1) * CH].astype(f32)
            du = pdo_in[0, e, n] + mm(k * w, ds_out)
            y = mm(inv[0, e, n].T, du)
            do_y = jnp.concatenate([do, y], axis=0)
            by_u = mm_nt(do_y, u)
            by_s = mm_nt(do_y, st)
            dp, dl = by_u[:CH], -by_u[CH:]
            dos, z = by_s[:CH], -by_s[CH:]
            dkw = mm_nt(u, ds_out)
            strict = jnp.where(row > col, decay, 0.0)
            bk = strict * kk_in[0, n]
            dlb = dl * bk
            f = dp * p + beta * dlb
            zk = z * k
            wk = w * (dkw * k)
            bs = beta * s
            dbeta = rowsum(y * v + s * zk + dlb)
            extra = jnp.sum(rowsum(wk + s_last * (ds_out * st)), axis=0, keepdims=True)
            dc = rowsum((f - f.T) + s * (do * qs) + bs * zk - wk)
            dc = dc + jnp.where(row[:, :1] == CH - 1, extra, 0.0)
            packed = jnp.where(col == 2 * e, dbeta, packed)
            packed = jnp.where(col == 2 * e + 1, dc, packed)
            dqk_sum = dqk_sum + dp * decay
            dkk_sum = dkk_sum + dl * (beta * strict)
            dq = dq + s * dos
            dk = dk + w * dkw + bs * z
            dvs[n, e] = beta * y
            if n > 0:
                grads[e] = mm(q_t * s_r, do) + s_last * ds_out - mm(k_t * (beta_r * s_r), y)
        dqs[n] = dq + mm(dqk_sum, k)
        dks[n] = dk + mm(dqk_sum.T, q) + mm(dkk_sum + dkk_sum.T, k)
        row_grads[0, n] = packed.T[: row_grads.shape[2]]
    dq = jnp.concatenate(dqs, axis=0)
    dk = jnp.concatenate(dks, axis=0)
    dv = jnp.concatenate(
        [jnp.concatenate([dvs[n, e] for e in range(heads)], axis=1) for n in range(blocks)], axis=0
    )
    daq = norm_back(dq, a_q[...], SCALE)
    dak = norm_back(dk, a_k[...], 1.0)
    dav = dv * (v_sig + v_all * (1.0 - v_sig))
    for da, taps, grad, end, spill in (
        (daq, q_taps, q_grad, q_end, q_spill),
        (dak, k_taps, k_grad, k_end, k_spill),
        (dav, v_taps, v_grad, v_end, v_spill),
    ):
        full = conv_back(da, taps, masks)
        grad[...] = full[:tokens].astype(bf16)
        end[...] = full[tokens - HALO : tokens]
        spill[...] = full[tokens:]


def shifted(array, by):
    peers = lax.axis_size(SEQ)
    return lax.ppermute(array, SEQ, [(i, i + by) for i in range(peers) if 0 <= i + by < peers])


def tri(upper):
    i = jnp.arange(CH)
    return ((i[:, None] <= i[None, :]) if upper else (i[:, None] >= i[None, :])).astype(f32)


def sds(shape, dtype=f32):
    return jax.ShapeDtypeStruct(shape, dtype)


def body(
    q_raw, k_raw, v_raw, beta_logit, gate_logit, out_grad, conv_q, conv_k, conv_v, a_log, dt_bias, doc_ids, swap_blocks
):
    tokens = q_raw.shape[0]
    blocks = tokens // CH
    hk = q_raw.shape[1] // DK
    hv = v_raw.shape[1] // DK
    rep = hv // hk
    shards = lax.axis_size(SEQ)
    hops = max(1, shards // DOC_PARTS)
    core = lax.axis_index("pair")
    swap = swap_blocks[0]
    flags = jnp.stack([jnp.where(core == 1, swap, 0), jnp.where(core == 0, swap, 0)]).astype(jnp.int32)

    start = jnp.where(core == 0, SWAP, 0)
    logits = jnp.concatenate([beta_logit, gate_logit], axis=0)
    bg_send = lax.dynamic_slice_in_dim(logits, start, SWAP, 1)
    send = jnp.concatenate(
        [lax.dynamic_slice_in_dim(x, start, SWAP, 0) for x in (q_raw, k_raw, v_raw, out_grad)], axis=1
    )
    got, bg_got = lax.ppermute((send, bg_send), "pair", [(0, 1), (1, 0)])
    ids_col = jnp.broadcast_to((doc_ids[tokens - HALO :] + 1).astype(bf16)[:, None], (HALO, CH))
    tail = jnp.concatenate([x[tokens - HALO :] for x in (q_raw, k_raw, v_raw)] + [ids_col], axis=1)
    before = shifted(tail, 1)
    own = jnp.concatenate([x[SWAP - HALO : SWAP] for x in (q_raw, k_raw, v_raw)], axis=1)
    chans = own.shape[1]
    halo = jnp.where(flags[0] > 0, own, before[:, :chans]).astype(f32)
    qw = hk * DK

    first = jnp.where(flags[0] > 0, bg_got, logits[:, :SWAP])
    second = jnp.where(flags[1] > 0, bg_got, logits[:, SWAP:])
    logits = jnp.concatenate([first, second], axis=1).astype(f32)
    beta = jax.nn.sigmoid(logits[:hv])
    gate = logits[hv:] + dt_bias[:, None]
    rate = -jnp.exp(a_log)[:, None]
    decay_log = rate * jax.nn.softplus(gate)
    c = jnp.dot(decay_log.reshape(hv * blocks, CH), tri(True), precision=highest).reshape(hv, blocks, CH)
    ids = doc_ids.astype(f32) + 1.0
    ext_ids = jnp.concatenate([before[:, chans].astype(f32), ids])
    doc = ids.reshape(blocks, CH)
    doc_before = ext_ids[HALO - 1 : HALO - 1 + tokens : CH]
    s = jnp.where(doc == doc_before[:, None], jnp.exp(c), 0.0)
    w = jnp.where(doc == doc[:, CH - 1 :], jnp.exp(jnp.minimum(c[:, :, CH - 1 :] - c, 0.0)), 0.0)
    rows = jnp.stack([beta.reshape(hv, blocks, CH), c, s, w], axis=2)
    rows = rows.reshape(hk, rep, blocks, 4, CH).transpose(0, 2, 1, 3, 4).reshape(hk, blocks, rep * 4, CH)
    docs = ((doc[:, :, None] == doc[:, None, :]) & (tri(False) > 0)[None]).astype(f32)
    masks = jnp.stack(
        [
            jnp.broadcast_to((ext_ids[HALO - d : HALO - d + tokens] == ids).astype(f32)[:, None], (tokens, CH))
            for d in range(1, TAPS)
        ]
    )
    taps = [x.astype(f32) for x in (conv_q, conv_k, conv_v)]

    vw = rep * DK
    col = lambda rows_, width, off=0: pl.BlockSpec((rows_, width), lambda i, off=off, width=width: (0, off // width + i))
    fixed = lambda shape: pl.BlockSpec(shape, lambda i: (0,) * len(shape))
    per = lambda shape: pl.BlockSpec(shape, lambda i: (i,) + (0,) * (len(shape) - 1))
    taps_specs = [col(TAPS, DK), col(TAPS, DK), col(TAPS, vw)]
    common_specs = taps_specs + [
        fixed((TAPS - 1, tokens, CH)),
        fixed((blocks, CH, CH)),
        per((1, blocks, rep * 4, CH)),
    ]
    params = pltpu.CompilerParams(dimension_semantics=("arbitrary",), vmem_limit_bytes=48 * 2**20)
    saved_specs = [
        col(tokens, DK), col(tokens, DK), col(tokens, vw), col(tokens, DK), col(tokens, DK), col(tokens, vw),
        per((1, rep, blocks, CH, CH)), per((1, blocks, CH, CH)), per((1, blocks, CH, CH)),
        per((1, rep, blocks, CH, CH)),
    ]
    saved_shapes = [
        sds((tokens, qw)), sds((tokens, qw)), sds((tokens, hv * DK)), sds((tokens, qw)), sds((tokens, qw)),
        sds((tokens, hv * DK), bf16), sds((hk, rep, blocks, CH, CH)), sds((hk, blocks, CH, CH)),
        sds((hk, blocks, CH, CH)), sds((hk, rep, blocks, CH, CH)),
    ]
    state_spec = per((rep, DK, DK))
    state_shape = sds((hv, DK, DK))
    units = hv * blocks * 2 * 4 * CH**3
    inputs = (flags, q_raw, k_raw, v_raw, out_grad, got, got, got, got, halo, halo, halo, *taps, masks, docs, rows)
    in_specs = [
        pl.BlockSpec(memory_space=pltpu.SMEM),
        col(tokens, DK), col(tokens, DK), col(tokens, vw), col(tokens, vw),
        col(SWAP, DK), col(SWAP, DK, qw), col(SWAP, vw, 2 * qw), col(SWAP, vw, 2 * qw + hv * DK),
        col(HALO, DK), col(HALO, DK, qw), col(HALO, vw, 2 * qw),
    ] + common_specs
    prepare_cost = pl.CostEstimate(flops=22 * units, bytes_accessed=24 * 2**20, transcendentals=2**20)
    if shards // DOC_PARTS == lax.axis_size("pair"):

        def held(spec, lag):
            if spec.index_map is None:
                return spec
            index = spec.index_map
            return pl.BlockSpec(spec.block_shape, lambda i: index(jnp.clip(i - lag, 0, hk - 1)))

        sems = pltpu.SemaphoreType.DMA((hk,))
        states = pltpu.VMEM((hk, rep, DK, DK), f32)
        prepared = pl.pallas_call(
            functools.partial(exchange_kernel, lax.axis_size("ctx"), hk),
            grid=(hk + 3,),
            in_specs=[held(spec, 0) for spec in in_specs],
            out_specs=[held(spec, 0) for spec in saved_specs] + [held(state_spec, 3)] * 2,
            out_shape=saved_shapes + [state_shape] * 2,
            scratch_shapes=[pltpu.VMEM((hk, 2, rep, DK, DK), f32)] * 2 + [states] * 5 + [sems] * 6,
            compiler_params=pltpu.CompilerParams(
                dimension_semantics=("arbitrary",), vmem_limit_bytes=48 * 2**20, collective_id=0,
                has_side_effects=True,
            ),
            cost_estimate=prepare_cost,
            name="exchange",
        )(*inputs)
        saved, (s_in, d_in) = prepared[:10], prepared[10:]
    else:
        prepared = pl.pallas_call(
            prepare_kernel,
            grid=(hk,),
            in_specs=in_specs,
            out_specs=saved_specs + [state_spec] * 3,
            out_shape=saved_shapes + [state_shape] * 3,
            compiler_params=params,
            cost_estimate=prepare_cost,
            name="prepare",
        )(*inputs)
        saved, (m, a, g) = prepared[:10], prepared[10:]
        join = pl.pallas_call(
            join_kernel,
            grid=(hk,),
            in_specs=[state_spec] * 5,
            out_specs=[state_spec] * 2,
            out_shape=[state_shape] * 2,
            compiler_params=params,
            cost_estimate=pl.CostEstimate(flops=hv * 16 * CH**3, bytes_accessed=7 * 2**20, transcendentals=0),
            name="join",
        )
        s_in, d_in = a, g
        for step in range(hops):
            s_in, d_in = shifted(s_in, 1), shifted(d_in, -1)
            if step < hops - 1:
                s_in, d_in = join(m, a, g, s_in, d_in)

    ends = [col(HALO, DK), col(HALO, DK), col(HALO, vw)]
    end_shapes = [sds((HALO, qw)), sds((HALO, qw)), sds((HALO, hv * DK))]
    results = pl.pallas_call(
        main_kernel,
        grid=(hk,),
        in_specs=saved_specs + common_specs + [state_spec] * 2,
        out_specs=[col(tokens, vw), col(tokens, DK), col(tokens, DK), col(tokens, vw)] + ends + ends + [per((1, blocks, 8, CH))],
        out_shape=[
            sds((tokens, hv * DK), bf16), sds((tokens, qw), bf16), sds((tokens, qw), bf16), sds((tokens, hv * DK), bf16)
        ] + end_shapes + end_shapes + [sds((hk, blocks, 8, CH))],
        compiler_params=params,
        cost_estimate=pl.CostEstimate(flops=17 * units, bytes_accessed=24 * 2**20, transcendentals=2**20),
        name="main",
    )(*saved, *taps, masks, docs, rows, s_in, d_in)
    layer_out, q_grad, k_grad, v_grad = results[:4]
    spilled = shifted(jnp.concatenate(results[7:10], axis=1), -1)
    ends_out = []
    at = 0
    for grad, end in zip((q_grad, k_grad, v_grad), results[4:7]):
        width = end.shape[1]
        last = (end + spilled[:, at : at + width]).astype(bf16)
        ends_out.append(lax.dynamic_update_slice(grad, last, (tokens - HALO, 0)))
        at += width
    rg = results[10][:, :, : 2 * rep].reshape(hk, blocks, rep, 2, CH).transpose(3, 0, 2, 1, 4)
    dbeta = rg[0].reshape(hv, tokens)
    dg = jnp.dot(rg[1].reshape(hv * blocks, CH), tri(False), precision=highest).reshape(hv, tokens)
    beta_grad = dbeta * beta * (1.0 - beta)
    gate_grad = dg * rate * jax.nn.sigmoid(gate)
    return (layer_out, ends_out[0], ends_out[1], ends_out[2], beta_grad.astype(bf16), gate_grad.astype(bf16))


def solution(mesh):
    rows = P(("groups", "ctx", "pair"), "head")
    rates = P("head", ("groups", "ctx", "pair"))
    taps = P(None, "head")
    return jax.shard_map(
        body,
        mesh=mesh,
        in_specs=(
            rows, rows, rows, rates, rates, rows, taps, taps, taps, P("head"), P("head"),
            P(("groups", "ctx", "pair")), P(("groups", "ctx")),
        ),
        out_specs=(rows, rows, rows, rows, rates, rates),
        check_vma=False,
    )
```

time: 1330 us -> 111 us (0.08)
  other arithmetic: 723 us -> 3.74 us
  matrix products: 233 us -> 0.26 us
  waiting for transfers between devices: 207 us -> 3.53 us
  local copies, waits for them, and re-layouts: 112 us -> 7.88 us
  Pallas kernels: 0 us -> 86.3 us
  starting transfers between devices: 23.2 us -> 7.13 us
  between operations: 16.6 us -> 1.66 us
    another operation x9 -> x4, other arithmetic: 639 us -> 0.29 us  [the longest x2 0.18 us: body(): rows = jnp.stack([beta.reshape(hv, blocks, CH), c, s, w], axis=2)]
    dot_general x72 -> x2, matrix products: 210 us -> 0.26 us  [the longest x1 0.13 us: body(): jnp.dot(decay_log.reshape(hv * blocks, CH), tri(True), precision=highest)]
    all_gather x4 -> x0, waiting for transfers between devices: 200 us -> none  [carried_in(): pieces = jax.tree.map(lambda part: lax.all_gather(part, axis), value)]
    pallas_call x0 -> x2, Pallas kernels: none -> 86.3 us  [the longest x1 53.3 us: body(): pl.pallas_call(functools.partial(exchange_kernel, lax.axis_size('ctx'), h...]
    another operation x16 -> x5, local copies, waits for them, and re-layouts: 25.5 us -> 0.31 us  [the longest x3 0.28 us: body(): jnp.stack([jnp.broadcast_to((ext_ids[HALO - d:HALO - d + tokens] == ids)....]
    another operation x4 -> x0, matrix products: 23.2 us -> none  [lower_solve(): jax.scipy.linalg.solve_triangular(strict_lower, right_side, lower=True, u...]
    while x162 -> x0, local copies, waits for them, and re-layouts: 21.6 us -> none
    reduce_sum x7 -> x0, other arithmetic: 17.1 us -> none  [the longest x1 4.08 us: span_pieces(): (beta_rate * start_decay)[:, None] * key_rows]
  transfers between devices with their start and end apart: 17 -> 4, of which waited for: 5 -> 2; matrix products, arithmetic and copies ran while one was open for 38% -> 7% of each run, Pallas kernels for 0% -> 0%
where the time goes in v1:
time: 111 us
  Pallas kernels  86.3 us (78%)
  local copies, waits for them, and re-layouts  7.88 us (7%)
  starting transfers between devices  7.13 us (6%)
  other arithmetic  3.74 us (3%)
  waiting for transfers between devices  3.53 us (3%)
  between operations  1.66 us (1%)
    pallas_call x1, Pallas kernels, body(): pl.pallas_call(functools.partial(exchange_kernel, lax.axis_size('ctx'), h...  53.3 us
    pallas_call x1, Pallas kernels, body(): pl.pallas_call(main_kernel, grid=(hk,), in_specs=saved_specs + common_spe...  33.1 us
    ppermute x2, starting transfers between devices, shifted(): lax.ppermute(array, SEQ, [(i, i + by) for i in range(peers) if 0 <= i + b...  7 us
    ppermute x2, waiting for transfers between devices, shifted(): lax.ppermute(array, SEQ, [(i, i + by) for i in range(peers) if 0 <= i + b...  3.12 us
    unnamed x21, local copies, waits for them, and re-layouts  2.37 us
  transfers between devices with their start and end apart: 4, of which 2 were waited for; matrix products, arithmetic and copies ran while one was open for 7% of the time, Pallas kernels for 0%

profile of v1, /device:TPU:1, one launch (start us, length us, event | category | flops | bytes accessed | tf_op | source)
XLA Modules:
  0.0 110.5 jit_solution(15014679336029923798)
XLA Ops:
  0.6 0.8 constant_dynamic-update-slice_fusion.1
  1.4 0.7 constant_dynamic-update-slice_fusion
  2.2 0.8 add_convert_fusion
  2.9 0.8 fusion.16
  3.7 0.8 fusion.17
  4.6 4.5 %collective-permute-start.1 = (bf16[8,4224]{1,0:T(8,128)(2,1)S(1)}, bf16[8,4224]{1,0:T(8,128)(2,1)S(1)}, u32[]{:S(2)}, u32[]{:S(2)}) collective-permute-start(bf16[8,4224]{1,0:T(8,128)(2,1)S(1)} %pad_maximum_fusion.3), channel_id=1, source_target_pairs={{0,1},{1,4},{4,5},{5,8},{8,9},{9,12},{12,13},{2,3},{3,6},{6,7},{7,... | collective-permute-start | bytes 202760 | tf_op jit(solution)/shard_map/ppermute | solution.py:406
  9.1 1.1 constant_dynamic-slice_fusion.2
  10.2 1.1 constant_dynamic-slice_fusion.3
  11.4 0.1 pad_maximum_fusion
  11.7 0.3 copy-done.5
  12.7 0.2 slice_reduce_fusion.1
  13.3 0.1 fusion.3
  13.4 0.2 slice_reduce_fusion
  13.6 0.1 copy.39
  14.8 0.4 collective-permute-done.refs_5_.refs_6_.refs_7_.refs_8_
  15.2 53.3 %exchange.1 = (f32[256,1024]{1,0:T(8,128)S(1)}, f32[256,1024]{1,0:T(8,128)S(1)}, f32[256,2048]{1,0:T(8,128)}, f32[256,1024]{1,0:T(8,128)S(1)}, f32[256,1024]{1,0...) custom-call(s32[2]{0:T(128)S(1)} %pad_add_fusion.refs_0_, ...), custom_call_target="tpu_custom_call" | custom-call | flops 11811160064 | bytes 25165824 | tf_op jit(solution)/shard_map/exchange/pallas_call | solution.py:514
  68.5 1.2 %copy-done.2 = bf16[256,2048]{1,0:T(8,128)(2,1)S(1)} copy-done((bf16[256,2048]{1,0:T(8,128)(2,1)S(1)}, bf16[256,2048]{1,0:T(8,128)(2,1)}, u32[]{:S(2)}) %copy-start.2) | copy-done | bytes 1048600
  69.7 33.1 %main.1 = (bf16[256,2048]{1,0:T(8,128)(2,1)}, bf16[256,1024]{1,0:T(8,128)(2,1)}, bf16[256,1024]{1,0:T(8,128)(2,1)}, bf16[256,2048]{1,0:T(8,128)(2,1)}, f32[8,102...) custom-call(f32[256,1024]{1,0:T(8,128)S(1)} %get-tuple-element.29.a_, ...), custom_call_target="tpu_custom_call" | custom-call | flops 9126805504 | bytes 25165824 | tf_op jit(solution)/shard_map/main/pallas_call | solution.py:559
  102.8 0.1 fusion.2
  103.0 2.5 %collective-permute-start.3 = (f32[8,4096]{1,0:T(8,128)S(1)}, f32[8,4096]{1,0:T(8,128)S(1)}, u32[]{:S(2)}, u32[]{:S(2)}) collective-permute-start(f32[8,4096]{1,0:T(8,128)S(1)} %pad_maximum_fusion.2), channel_id=1, source_target_pairs={{1,0},{4,1},{5,4},{8,5},{9,8},{12,9},{13,12},{3,2},{6,3},{7,6},{10... | collective-permute-start | bytes 393224 | tf_op jit(solution)/shard_map/ppermute | solution.py:406
  105.5 0.7 multiply_convert_fusion
  106.2 3.1 %collective-permute-done.3 = f32[8,4096]{1,0:T(8,128)S(1)} collective-permute-done((f32[8,4096]{1,0:T(8,128)S(1)}, f32[8,4096]{1,0:T(8,128)S(1)}, u32[]{:S(2)}, u32[]{:S(2)}) %collective-permute-start.3) | collective-permute-done | bytes 131104 | tf_op jit(solution)/shard_map/ppermute | solution.py:406
  109.3 0.6 fusion.4
  109.9 0.6 fusion.8
  (57 shorter events, 1.7 us)
Async XLA Ops:
  0.6 10.7 %copy-start.3 = (bf16[256,2048]{1,0:T(8,128)(2,1)S(1)}, bf16[256,2048]{1,0:T(8,128)(2,1)}, u32[]{:S(2)}) copy-start(bf16[256,2048]{1,0:T(8,128)(2,1)} %refs_4_.1) | copy-start | bytes 3145732
  2.1 11.0 %collective-permute-start.2 = (bf16[32,128]{1,0:T(8,128)(2,1)S(1)}, bf16[32,128]{1,0:T(8,128)(2,1)S(1)}, u32[]{:S(2)}, u32[]{:S(2)}) collective-permute-start(bf16[32,128]{1,0:T(8,128)(2,1)S(1)} %constant_dynamic-slice_fusion), channel_id=1, source_target_pairs={{0,1},{1,0},{2,3},{3,2},{4,5},{5,4},{6,7},{7,6},{8,9},{9,8},{10,11... | collective-permute-start | bytes 24584 | tf_op jit(solution)/shard_map/ppermute | solution.py:438
  4.6 9.2 %collective-permute-start.1 = (bf16[8,4224]{1,0:T(8,128)(2,1)S(1)}, bf16[8,4224]{1,0:T(8,128)(2,1)S(1)}, u32[]{:S(2)}, u32[]{:S(2)}) collective-permute-start(bf16[8,4224]{1,0:T(8,128)(2,1)S(1)} %pad_maximum_fusion.3), channel_id=1, source_target_pairs={{0,1},{1,4},{4,5},{5,8},{8,9},{9,12},{12,13},{2,3},{3,6},{6,7},{7,... | collective-permute-start | bytes 202760 | tf_op jit(solution)/shard_map/ppermute | solution.py:406
  11.3 0.7 copy-start.5
  11.3 1.4 %copy-start.9 = (f32[16]{0:T(128)S(1)}, f32[16]{0:T(128)}, u32[]{:S(2)}) copy-start(f32[16]{0:T(128)} %param.22) | copy-start | bytes 196
  11.3 1.7 %copy-start.6 = (bf16[4,1024]{1,0:T(4,128)(2,1)S(1)}, bf16[4,1024]{1,0:T(4,128)(2,1)}, u32[]{:S(2)}) copy-start(bf16[4,1024]{1,0:T(4,128)(2,1)} %param.19) | copy-start | bytes 24580
  11.3 1.7 %copy-start.7 = (bf16[4,1024]{1,0:T(4,128)(2,1)S(1)}, bf16[4,1024]{1,0:T(4,128)(2,1)}, u32[]{:S(2)}) copy-start(bf16[4,1024]{1,0:T(4,128)(2,1)} %param.20) | copy-start | bytes 24580
  11.3 1.7 %copy-start.4 = (bf16[4,2048]{1,0:T(4,128)(2,1)S(1)}, bf16[4,2048]{1,0:T(4,128)(2,1)}, u32[]{:S(2)}) copy-start(bf16[4,2048]{1,0:T(4,128)(2,1)} %param.21) | copy-start | bytes 49156
  11.4 1.8 %copy-start.8 = (f32[16]{0:T(128)S(1)}, f32[16]{0:T(128)}, u32[]{:S(2)}) copy-start(f32[16]{0:T(128)} %param.23) | copy-start | bytes 196
  11.4 3.8 %copy-start = (bf16[256,1024]{1,0:T(8,128)(2,1)S(1)}, bf16[256,1024]{1,0:T(8,128)(2,1)}, u32[]{:S(2)}) copy-start(bf16[256,1024]{1,0:T(8,128)(2,1)} %refs_1_.1) | copy-start | bytes 1572868
  11.4 3.8 %copy-start.1 = (bf16[256,1024]{1,0:T(8,128)(2,1)S(1)}, bf16[256,1024]{1,0:T(8,128)(2,1)}, u32[]{:S(2)}) copy-start(bf16[256,1024]{1,0:T(8,128)(2,1)} %refs_2_.1) | copy-start | bytes 1572868
  11.6 3.6 %collective-permute-start = (bf16[128,6144]{1,0:T(8,128)(2,1)S(1)}, bf16[128,6144]{1,0:T(8,128)(2,1)}, u32[]{:S(2)}, u32[]{:S(2)}) collective-permute-start(bf16[128,6144]{1,0:T(8,128)(2,1)S(1)} %pad_maximum_fusion), channel_id=1, source_target_pairs={{0,1},{1,0},{2,3},{3,2},{4,5},{5,4},{6,7},{7,6},{8,9},{9,8},{10,11... | collective-permute-start | bytes 4718600 | tf_op jit(solution)/shard_map/ppermute | solution.py:438
  68.5 1.2 %copy-start.2 = (bf16[256,2048]{1,0:T(8,128)(2,1)S(1)}, bf16[256,2048]{1,0:T(8,128)(2,1)}, u32[]{:S(2)}) copy-start(bf16[256,2048]{1,0:T(8,128)(2,1)} %get-tuple-element.34.seq_grad) | copy-start | bytes 3145732
  103.0 6.3 %collective-permute-start.3 = (f32[8,4096]{1,0:T(8,128)S(1)}, f32[8,4096]{1,0:T(8,128)S(1)}, u32[]{:S(2)}, u32[]{:S(2)}) collective-permute-start(f32[8,4096]{1,0:T(8,128)S(1)} %pad_maximum_fusion.2), channel_id=1, source_target_pairs={{1,0},{4,1},{5,4},{8,5},{9,8},{12,9},{13,12},{3,2},{6,3},{7,6},{10... | collective-permute-start | bytes 393224 | tf_op jit(solution)/shard_map/ppermute | solution.py:406

commit v2 on v1

--- a/solution.py
+++ b/solution.py
@@ -38,6 +38,25 @@
     r = lax.dot_general(lhs, rhs, (((1,), (0,)), ((), ())), preferred_element_type=f32)
     n = b.shape[1]
     return r[:, :n] + r[:, n:]
+
+
+def mm_half(a, b):
+    return lax.dot_general(
+        jnp.concatenate(split(a), axis=1), jnp.concatenate([b, b], axis=0), (((1,), (0,)), ((), ())),
+        preferred_element_type=f32,
+    )
+
+
+def odd_blocks(x, size):
+    return jnp.concatenate([x[i : i + size] for i in range(size, CH, 2 * size)], axis=0)
+
+
+def with_odd(even, odd, size):
+    parts = []
+    for i in range(0, CH // 2, size):
+        parts.append(jnp.zeros((size, CH), odd.dtype) if even is None else even[2 * i : 2 * i + size])
+        parts.append(odd[i : i + size])
+    return jnp.concatenate(parts, axis=0)
 
 
 def mm_nt(a, b):
@@ -118,7 +137,7 @@
     a_v[...] = va
     gs = fetch(g_raw, g_got, flags)
     seq_grad[...] = gs
-    do_all = gs.astype(f32)
+    do_all = gs
     qu = qa * sigmoid(qa)
     ku = ka * sigmoid(ka)
     v_all = va * sigmoid(va)
@@ -155,14 +174,21 @@
     size = 1
     while (2 << size) <= CH:
         near = ((row >> (size + 1)) == (col >> (size + 1))) & ((row >> size) != (col >> size))
-        half = [mm(jnp.where(near, item[2], 0.0), t) for item, t in zip(state, inv)]
-        inv = [t - mm(t, h) for t, h in zip(inv, half)]
+        width = 1 << size
+        if width < 8:
+            half = [mm(jnp.where(near, item[2], 0.0), t) for item, t in zip(state, inv)]
+            inv = [t - mm(t, h) for t, h in zip(inv, half)]
+        else:
+            half = [mm(odd_blocks(jnp.where(near, item[2], 0.0), width), t) for item, t in zip(state, inv)]
+            odds = [odd_blocks(t, width) for t in inv]
+            odds = [t - mm(t, with_odd(None, h, width)) for t, h in zip(odds, half)]
+            inv = [with_odd(t, o, width) for t, o in zip(inv, odds)]
         size += 1
     maps = {}
     for item, t in zip(state, inv):
         n, e, low, p, do, v, kw, bsk_t, bsk, sq_t, bv, s_last = item
         inv_out[0, e, n] = t
-        pdo = mm(p.T, do)
+        pdo = mm_half(p.T, do)
         pdo_out[0, e, n] = pdo
         t_t = t.T
         b = mm(t_t, kw)
@@ -170,7 +196,7 @@
         b_t = b.T
         m = s_last * eye - mm(b_t, bsk)
         a = mm(b_t, bv)
-        g = mm(sq_t, do) - mm(bsk_t, cc)
+        g = mm_half(sq_t, do) - mm(bsk_t, cc)
         maps[n, e] = (m, a, g)
     results = []
     for e in range(heads):
@@ -350,7 +376,8 @@
             s_last = s_r[:, CH - 1 :]
             st, u, qs, decay, p, v = fwd[n, e]
             ds_out = grads[e]
-            do = seq_grad[n * CH : (n + 1) * CH, e * CH : (e + 1) * CH].astype(f32)
+            do_half = seq_grad[n * CH : (n + 1) * CH, e * CH : (e + 1) * CH]
+            do = do_half.astype(f32)
             du = pdo_in[0, e, n] + mm(k * w, ds_out)
             y = mm(inv[0, e, n].T, du)
             do_y = jnp.concatenate([do, y], axis=0)
@@ -378,7 +405,7 @@
             dk = dk + w * dkw + bs * z
             dvs[n, e] = beta * y
             if n > 0:
-                grads[e] = mm(q_t * s_r, do) + s_last * ds_out - mm(k_t * (beta_r * s_r), y)
+                grads[e] = mm_half(q_t * s_r, do_half) + s_last * ds_out - mm(k_t * (beta_r * s_r), y)
         dqs[n] = dq + mm(dqk_sum, k)
         dks[n] = dk + mm(dqk_sum.T, q) + mm(dkk_sum + dkk_sum.T, k)
         row_grads[0, n] = packed.T[: row_grads.shape[2]]
@@ -435,9 +462,13 @@
     send = jnp.concatenate(
         [lax.dynamic_slice_in_dim(x, start, SWAP, 0) for x in (q_raw, k_raw, v_raw, out_grad)], axis=1
     )
-    got, bg_got = lax.ppermute((send, bg_send), "pair", [(0, 1), (1, 0)])
-    ids_col = jnp.broadcast_to((doc_ids[tokens - HALO :] + 1).astype(bf16)[:, None], (HALO, CH))
-    tail = jnp.concatenate([x[tokens - HALO :] for x in (q_raw, k_raw, v_raw)] + [ids_col], axis=1)
+    got = lax.ppermute(send, "pair", [(0, 1), (1, 0)])
+    send, bg_send, tail_ids, tails = lax.optimization_barrier(
+        (send, bg_send, doc_ids[tokens - HALO :], [x[tokens - HALO :] for x in (q_raw, k_raw, v_raw)])
+    )
+    bg_got = lax.ppermute(bg_send, "pair", [(0, 1), (1, 0)])
+    ids_col = jnp.broadcast_to((tail_ids + 1).astype(bf16)[:, None], (HALO, CH))
+    tail = jnp.concatenate(tails + [ids_col], axis=1)
     before = shifted(tail, 1)
     own = jnp.concatenate([x[SWAP - HALO : SWAP] for x in (q_raw, k_raw, v_raw)], axis=1)
     chans = own.shape[1]

time: 111 us -> 108 us (0.973)
  local copies, waits for them, and re-layouts: 7.88 us -> 6.37 us
    unnamed x21 -> x23, local copies, waits for them, and re-layouts: 2.37 us -> 2.1 us
    dynamic_slice x3 -> x2, local copies, waits for them, and re-layouts: 2.2 us -> 2.35 us  [body(): lax.dynamic_slice_in_dim(x, start, SWAP, 0)]
  transfers between devices with their start and end apart: 4 -> 4, of which waited for: 2 -> 1; matrix products, arithmetic and copies ran while one was open for 7% -> 3% of each run, Pallas kernels for 0% -> 0%
where the time goes in v2:
time: 108 us
  Pallas kernels  85.9 us (80%)
  starting transfers between devices  7.26 us (7%)
  local copies, waits for them, and re-layouts  6.37 us (6%)
  waiting for transfers between devices  3.14 us (3%)
  other arithmetic  2.99 us (3%)
  between operations  1.68 us (2%)
    pallas_call x1, Pallas kernels, body(): pl.pallas_call(functools.partial(exchange_kernel, lax.axis_size('ctx'), h...  52.8 us
    pallas_call x1, Pallas kernels, body(): pl.pallas_call(main_kernel, grid=(hk,), in_specs=saved_specs + common_spe...  33.2 us
    ppermute x2, starting transfers between devices, shifted(): lax.ppermute(array, SEQ, [(i, i + by) for i in range(peers) if 0 <= i + b...  7.02 us
    ppermute x2, waiting for transfers between devices, shifted(): lax.ppermute(array, SEQ, [(i, i + by) for i in range(peers) if 0 <= i + b...  3.13 us
    dynamic_slice x2, local copies, waits for them, and re-layouts, body(): lax.dynamic_slice_in_dim(x, start, SWAP, 0)  2.35 us
  transfers between devices with their start and end apart: 4, of which 1 were waited for; matrix products, arithmetic and copies ran while one was open for 3% of the time, Pallas kernels for 0%

profile of v2, /device:TPU:1, one launch (start us, length us, event | category | flops | bytes accessed | tf_op | source)
XLA Modules:
  0.0 107.6 jit_solution(18395310575682794247)
XLA Ops:
  0.6 1.1 constant_dynamic-slice_fusion.3
  1.7 1.3 %constant_dynamic-slice_fusion.1 = (bf16[128,2048]{1,0:T(8,128)(2,1)S(1)}, bf16[128,2048]{1,0:T(8,128)(2,1)S(1)}) fusion(bf16[256,2048]{1,0:T(8,128)(2,1)} %refs_4_.1, s32[]{:T(128)S(6)} %select_n.67, bf16[256,2048]{1,0:T(8,128)(2,1)} %refs_3_.1), kind=kLoop, calls=%fused_computation.45 | loop fusion | bytes 2097156 | tf_op jit(solution)/shard_map/dynamic_slice | solution.py:463
  3.1 0.1 pad_maximum_fusion
  3.2 0.1 collective-permute-start
  3.4 0.7 copy-done
  4.0 0.2 copy-done.1
  4.2 0.8 fusion.16
  5.1 0.1 collective-permute-start.2
  5.3 4.5 %collective-permute-start.1 = (bf16[8,4224]{1,0:T(8,128)(2,1)S(1)}, bf16[8,4224]{1,0:T(8,128)(2,1)S(1)}, u32[]{:S(2)}, u32[]{:S(2)}) collective-permute-start(bf16[8,4224]{1,0:T(8,128)(2,1)S(1)} %pad_maximum_fusion.3), channel_id=1, source_target_pairs={{0,1},{1,4},{4,5},{5,8},{8,9},{9,12},{12,13},{2,3},{3,6},{6,7},{7,... | collective-permute-start | bytes 202760 | tf_op jit(solution)/shard_map/ppermute | solution.py:433
  10.6 0.2 slice_reduce_fusion.1
  11.2 0.1 fusion.3
  11.3 0.2 slice_reduce_fusion
  11.5 0.1 copy.39
  11.7 0.1 convert_reduce_fusion
  12.0 0.1 fusion.20
  12.7 52.8 %exchange.1 = (f32[256,1024]{1,0:T(8,128)S(1)}, f32[256,1024]{1,0:T(8,128)S(1)}, f32[256,2048]{1,0:T(8,128)}, f32[256,1024]{1,0:T(8,128)S(1)}, f32[256,1024]{1,0...) custom-call(s32[2]{0:T(128)S(1)} %pad_add_fusion.refs_0_, ...), custom_call_target="tpu_custom_call" | custom-call | flops 11811160064 | bytes 25165824 | tf_op jit(solution)/shard_map/exchange/pallas_call | solution.py:545
  65.5 1.2 %copy-done.2 = bf16[256,2048]{1,0:T(8,128)(2,1)S(1)} copy-done((bf16[256,2048]{1,0:T(8,128)(2,1)S(1)}, bf16[256,2048]{1,0:T(8,128)(2,1)}, u32[]{:S(2)}) %copy-start.2) | copy-done | bytes 1048600
  66.7 33.2 %main.1 = (bf16[256,2048]{1,0:T(8,128)(2,1)}, bf16[256,1024]{1,0:T(8,128)(2,1)}, bf16[256,1024]{1,0:T(8,128)(2,1)}, bf16[256,2048]{1,0:T(8,128)(2,1)}, f32[8,102...) custom-call(f32[256,1024]{1,0:T(8,128)S(1)} %get-tuple-element.39.a_, ...), custom_call_target="tpu_custom_call" | custom-call | flops 9126805504 | bytes 25165824 | tf_op jit(solution)/shard_map/main/pallas_call | solution.py:590
  99.9 0.1 fusion.2
  100.1 2.5 %collective-permute-start.3 = (f32[8,4096]{1,0:T(8,128)S(1)}, f32[8,4096]{1,0:T(8,128)S(1)}, u32[]{:S(2)}, u32[]{:S(2)}) collective-permute-start(f32[8,4096]{1,0:T(8,128)S(1)} %pad_maximum_fusion.2), channel_id=1, source_target_pairs={{1,0},{4,1},{5,4},{8,5},{9,8},{12,9},{13,12},{3,2},{6,3},{7,6},{10... | collective-permute-start | bytes 393224 | tf_op jit(solution)/shard_map/ppermute | solution.py:433
  102.6 0.7 multiply_convert_fusion
  103.3 3.1 %collective-permute-done.3 = f32[8,4096]{1,0:T(8,128)S(1)} collective-permute-done((f32[8,4096]{1,0:T(8,128)S(1)}, f32[8,4096]{1,0:T(8,128)S(1)}, u32[]{:S(2)}, u32[]{:S(2)}) %collective-permute-start.3) | collective-permute-done | bytes 131104 | tf_op jit(solution)/shard_map/ppermute | solution.py:433
  106.4 0.6 fusion.4
  107.0 0.6 fusion.8
  (59 shorter events, 1.4 us)
Async XLA Ops:
  3.0 1.0 copy-start
  3.0 1.2 %copy-start.1 = (bf16[256,1024]{1,0:T(8,128)(2,1)S(1)}, bf16[256,1024]{1,0:T(8,128)(2,1)}, u32[]{:S(2)}) copy-start(bf16[256,1024]{1,0:T(8,128)(2,1)} %refs_2_.1) | copy-start | bytes 1572868
  3.0 2.0 %copy-start.4 = (s32[256]{0:T(256)S(1)}, s32[256]{0:T(256)}, u32[]{:S(2)}) copy-start(s32[256]{0:T(256)} %param.24) | copy-start | bytes 3076
  3.0 2.0 %copy-start.7 = (bf16[16,256]{1,0:T(8,128)(2,1)S(1)}, bf16[16,256]{1,0:T(8,128)(2,1)}, u32[]{:S(2)}) copy-start(bf16[16,256]{1,0:T(8,128)(2,1)} %param.16) | copy-start | bytes 24580
  3.0 2.0 %copy-start.8 = (bf16[16,256]{1,0:T(8,128)(2,1)S(1)}, bf16[16,256]{1,0:T(8,128)(2,1)}, u32[]{:S(2)}) copy-start(bf16[16,256]{1,0:T(8,128)(2,1)} %param.17) | copy-start | bytes 24580
  3.1 7.5 %copy-start.10 = (f32[16]{0:T(128)S(1)}, f32[16]{0:T(128)}, u32[]{:S(2)}) copy-start(f32[16]{0:T(128)} %param.22) | copy-start | bytes 196
  3.1 7.9 %copy-start.5 = (bf16[4,1024]{1,0:T(4,128)(2,1)S(1)}, bf16[4,1024]{1,0:T(4,128)(2,1)}, u32[]{:S(2)}) copy-start(bf16[4,1024]{1,0:T(4,128)(2,1)} %param.19) | copy-start | bytes 24580
  3.1 7.9 %copy-start.6 = (bf16[4,1024]{1,0:T(4,128)(2,1)S(1)}, bf16[4,1024]{1,0:T(4,128)(2,1)}, u32[]{:S(2)}) copy-start(bf16[4,1024]{1,0:T(4,128)(2,1)} %param.20) | copy-start | bytes 24580
  3.1 7.9 %copy-start.3 = (bf16[4,2048]{1,0:T(4,128)(2,1)S(1)}, bf16[4,2048]{1,0:T(4,128)(2,1)}, u32[]{:S(2)}) copy-start(bf16[4,2048]{1,0:T(4,128)(2,1)} %param.21) | copy-start | bytes 49156
  3.1 7.9 %copy-start.9 = (f32[16]{0:T(128)S(1)}, f32[16]{0:T(128)}, u32[]{:S(2)}) copy-start(f32[16]{0:T(128)} %param.23) | copy-start | bytes 196
  3.2 9.4 %collective-permute-start = (bf16[128,6144]{1,0:T(8,128)(2,1)S(1)}, bf16[128,6144]{1,0:T(8,128)(2,1)}, u32[]{:S(2)}, u32[]{:S(2)}) collective-permute-start(bf16[128,6144]{1,0:T(8,128)(2,1)S(1)} %pad_maximum_fusion), channel_id=1, source_target_pairs={{0,1},{1,0},{2,3},{3,2},{4,5},{5,4},{6,7},{7,6},{8,9},{9,8},{10,11... | collective-permute-start | bytes 4718600 | tf_op jit(solution)/shard_map/ppermute | solution.py:465
  5.1 5.9 %collective-permute-start.2 = (bf16[32,128]{1,0:T(8,128)(2,1)S(1)}, bf16[32,128]{1,0:T(8,128)(2,1)S(1)}, u32[]{:S(2)}, u32[]{:S(2)}) collective-permute-start(bf16[32,128]{1,0:T(8,128)(2,1)S(1)} %constant_dynamic-slice_fusion), channel_id=1, source_target_pairs={{0,1},{1,0},{2,3},{3,2},{4,5},{5,4},{6,7},{7,6},{8,9},{9,8},{10,11... | collective-permute-start | bytes 24584 | tf_op jit(solution)/shard_map/ppermute | solution.py:469
  5.3 6.4 %collective-permute-start.1 = (bf16[8,4224]{1,0:T(8,128)(2,1)S(1)}, bf16[8,4224]{1,0:T(8,128)(2,1)S(1)}, u32[]{:S(2)}, u32[]{:S(2)}) collective-permute-start(bf16[8,4224]{1,0:T(8,128)(2,1)S(1)} %pad_maximum_fusion.3), channel_id=1, source_target_pairs={{0,1},{1,4},{4,5},{5,8},{8,9},{9,12},{12,13},{2,3},{3,6},{6,7},{7,... | collective-permute-start | bytes 202760 | tf_op jit(solution)/shard_map/ppermute | solution.py:433
  65.5 1.2 %copy-start.2 = (bf16[256,2048]{1,0:T(8,128)(2,1)S(1)}, bf16[256,2048]{1,0:T(8,128)(2,1)}, u32[]{:S(2)}) copy-start(bf16[256,2048]{1,0:T(8,128)(2,1)} %get-tuple-element.44.seq_grad) | copy-start | bytes 3145732
  100.1 6.3 %collective-permute-start.3 = (f32[8,4096]{1,0:T(8,128)S(1)}, f32[8,4096]{1,0:T(8,128)S(1)}, u32[]{:S(2)}, u32[]{:S(2)}) collective-permute-start(f32[8,4096]{1,0:T(8,128)S(1)} %pad_maximum_fusion.2), channel_id=1, source_target_pairs={{1,0},{4,1},{5,4},{8,5},{9,8},{12,9},{13,12},{3,2},{6,3},{7,6},{10... | collective-permute-start | bytes 393224 | tf_op jit(solution)/shard_map/ppermute | solution.py:433
